TPU v7x, 32 devices: a whole 2x2x4 slice. The times are simulated.
32 devices in a mesh: dp: 4 (over x, core), row: 4 (over z), col: 2 (over y).
Axes of the slice: x: 2, y: 2, z: 4, core: 2. Of those that a mesh axis runs over, the one named last changes fastest.
Arguments:
- hidden_in: float32 [1024, 32768], P('col', ('dp', 'row')), may hold values from -6 to 6
- lengths: int32 [64], P(('dp', 'row')), may hold values from 1 to 512, as said below
- ln1_gain: float32 [1024], P('col'), may hold values from 0.25 to 1.75
- ln1_shift: float32 [1024], P('col'), may hold values from -3 to 3
- w_qkv: bfloat16 [1024, 3072], P('row', 'col'), may hold values from -0.1875 to 0.1875
- bias_q: float32 [1024], P('col'), may hold values from -3 to 3
- bias_v: float32 [1024], P('col'), may hold values from -3 to 3
- w_out: bfloat16 [1024, 1024], P('col', 'row'), may hold values from -0.375 to 0.375
- bias_out: float32 [1024], P('col'), may hold values from -3 to 3
- ln2_gain: float32 [1024], P('col'), may hold values from 0.25 to 1.75
- ln2_shift: float32 [1024], P('col'), may hold values from -3 to 3
- w_up: bfloat16 [1024, 4096], P('row', 'col'), may hold values from -0.1875 to 0.1875
- bias_up: float32 [4096], P('col'), may hold values from -3 to 3
- w_down: bfloat16 [4096, 1024], P('col', 'row'), may hold values from -0.125 to 0.125
- bias_down: float32 [1024], P('col'), may hold values from -3 to 3
- cotangent: float32 [1024, 32768], P('col', ('dp', 'row')), may hold values from -6 to 6
Outputs:
- hidden_out: float32 [1024, 32768], P('col', ('dp', 'row'))
- grad_in: float32 [1024, 32768], P('col', ('dp', 'row'))
- grad_ln1_gain: float32 [1024], P('col')
- grad_ln1_shift: float32 [1024], P('col')
- grad_w_qkv: float32 [1024, 3072], P('row', 'col')
- grad_bias_q: float32 [1024], P('col')
- grad_bias_v: float32 [1024], P('col')
- grad_w_out: float32 [1024, 1024], P('col', 'row')
- grad_bias_out: float32 [1024], P('col')
- grad_ln2_gain: float32 [1024], P('col')
- grad_ln2_shift: float32 [1024], P('col')
- grad_w_up: float32 [1024, 4096], P('row', 'col')
- grad_bias_up: float32 [4096], P('col')
- grad_w_down: float32 [4096, 1024], P('col', 'row')
- grad_bias_down: float32 [1024], P('col')
Inputs may be any that keep to these rules, and one draw needn't show every extreme that they name: `lengths`: each slot holds one sequence of this many tokens followed by padding; some slot of every index pair of dp and row is full.
All inputs are finite; a program needn't handle non-finite values.
Results may differ from a plain program's by a relative error of at most 0.019.
Values may be sent and summed in bfloat16 or wider, within the bound.
A program may use at most 192 MiB of HBM per device.

v0:
```python
from functools import partial
import jax
import jax.numpy as jnp
from jax import lax
from jax.sharding import PartitionSpec as P

HEADS = 16
HEAD = 64
EPS = 1e-05
NEG = -1e30


def norm_forward(value, gain, shift):
    width = value.shape[1] * lax.axis_size("col")
    sums = lax.psum((jnp.sum(value, axis=1), jnp.sum(value * value, axis=1)), "col")
    mean = (sums[0] / width)[:, None]
    var = (sums[1] / width)[:, None] - mean * mean
    inverse = lax.rsqrt(var + EPS)
    normed = (value - mean) * inverse
    return (normed, inverse, (normed * gain + shift).astype(jnp.bfloat16))


def norm_backward(incoming, normed, inverse, gain):
    width = incoming.shape[1] * lax.axis_size("col")
    scaled = incoming * gain
    sums = lax.psum((jnp.sum(scaled, axis=1), jnp.sum(scaled * normed, axis=1)), "col")
    return inverse * (scaled - sums[0][:, None] / width - normed * sums[1][:, None] / width)


def gather_rows(value):
    return lax.all_gather(value, "col", axis=1, tiled=True)


def back_columns(value):
    return lax.psum_scatter(
        value.astype(jnp.bfloat16), "col", scatter_dimension=1, tiled=True
    ).astype(jnp.float32)


def slot_scores(slopes, query, keys, length):
    span = query.shape[0]
    pos = jnp.arange(span)
    offset = (pos[None, :] - pos[:, None]).astype(jnp.float32)
    raw = jnp.einsum("qhd,khd->hqk", query, keys, preferred_element_type=jnp.float32) * 0.125
    raw = raw + slopes[:, None, None] * offset[None]
    visible = (pos[None, :] <= pos[:, None]) & (pos[None, :] < length)
    return jnp.where(visible[None], raw, NEG)


def forward_slot(slopes, item):
    query, keys, values, length = item
    scores = slot_scores(slopes, query, keys, length)
    top = jnp.max(scores, axis=-1, keepdims=True)
    expo = jnp.exp(scores - top)
    total = jnp.sum(expo, axis=-1, keepdims=True)
    probs = expo / total
    attended = jnp.einsum(
        "hqk,khd->qhd", probs.astype(jnp.bfloat16), values, preferred_element_type=jnp.float32
    )
    return (attended, (top + jnp.log(total))[..., 0])


def backward_slot(slopes, item):
    query, keys, values, grad_out, lse, length = item
    scores = slot_scores(slopes, query, keys, length)
    probs = jnp.exp(scores - lse[..., None])
    grad_probs = jnp.einsum("qhd,khd->hqk", grad_out, values, preferred_element_type=jnp.float32)
    grad_values = jnp.einsum(
        "hqk,qhd->khd", probs.astype(jnp.bfloat16), grad_out, preferred_element_type=jnp.float32
    )
    inner = jnp.sum(probs * grad_probs, axis=-1, keepdims=True)
    grad_scores = (probs * (grad_probs - inner)).astype(jnp.bfloat16)
    grad_query = (
        jnp.einsum("hqk,khd->qhd", grad_scores, keys, preferred_element_type=jnp.float32) * 0.125
    )
    grad_keys = (
        jnp.einsum("hqk,qhd->khd", grad_scores, query, preferred_element_type=jnp.float32) * 0.125
    )
    return (grad_query, grad_keys, grad_values)


def body(
    hidden_in,
    lengths,
    ln1_gain,
    ln1_shift,
    w_qkv,
    bias_q,
    bias_v,
    w_out,
    bias_out,
    ln2_gain,
    ln2_shift,
    w_up,
    bias_up,
    w_down,
    bias_down,
    cotangent,
):
    tokens_in = jnp.transpose(hidden_in)
    grad_given = jnp.transpose(cotangent)
    rows = tokens_in.shape[0]
    slots = lengths.shape[0]
    span = rows // slots
    heads_here = w_qkv.shape[1] // (3 * HEAD)
    head_ids = lax.axis_index("col") * heads_here + jnp.arange(heads_here)
    slopes = jnp.exp2(-8.0 * (head_ids.astype(jnp.float32) + 1.0) / HEADS)
    qkv_full, up_full, out_full, down_full = (
        lax.all_gather(w_qkv, "row", axis=0, tiled=True),
        lax.all_gather(w_up, "row", axis=0, tiled=True),
        lax.all_gather(w_out, "row", axis=1, tiled=True),
        lax.all_gather(w_down, "row", axis=1, tiled=True),
    )
    normed1, inverse1, low1 = norm_forward(tokens_in, ln1_gain, ln1_shift)
    rows1 = gather_rows(low1)
    mixed = jnp.dot(rows1, qkv_full, preferred_element_type=jnp.float32).reshape(
        rows, heads_here, 3, HEAD
    )
    query = (
        (mixed[:, :, 0] + bias_q.reshape(heads_here, HEAD))
        .astype(jnp.bfloat16)
        .reshape(slots, span, heads_here, HEAD)
    )
    keys = mixed[:, :, 1].astype(jnp.bfloat16).reshape(slots, span, heads_here, HEAD)
    values = (
        (mixed[:, :, 2] + bias_v.reshape(heads_here, HEAD))
        .astype(jnp.bfloat16)
        .reshape(slots, span, heads_here, HEAD)
    )
    attended, lse = lax.map(partial(forward_slot, slopes), (query, keys, values, lengths))
    attn_low = attended.reshape(rows, heads_here * HEAD).astype(jnp.bfloat16)
    projected = lax.psum_scatter(
        jnp.dot(attn_low, out_full, preferred_element_type=jnp.float32),
        "col",
        scatter_dimension=1,
        tiled=True,
    )
    hidden1 = tokens_in + projected + bias_out
    normed2, inverse2, low2 = norm_forward(hidden1, ln2_gain, ln2_shift)
    rows2 = gather_rows(low2)
    pre = jnp.dot(rows2, up_full, preferred_element_type=jnp.float32) + bias_up
    act, act_pull = jax.vjp(partial(jax.nn.gelu, approximate=True), pre)
    act_low = act.astype(jnp.bfloat16)
    down_terms = jnp.dot(act_low, down_full, preferred_element_type=jnp.float32)
    result = (
        hidden1
        + lax.psum_scatter(
            down_terms.astype(jnp.bfloat16), "col", scatter_dimension=1, tiled=True
        ).astype(jnp.float32)
        + bias_down
    )
    grad_low = grad_given.astype(jnp.bfloat16)
    grad_full = lax.all_gather(grad_low, "col", axis=1, tiled=True)
    grad_down = jnp.einsum("tf,td->fd", act_low, grad_full, preferred_element_type=jnp.float32)
    grad_act = jnp.einsum("td,fd->tf", grad_full, down_full, preferred_element_type=jnp.float32)
    grad_pre = act_pull(grad_act)[0]
    grad_pre_low = grad_pre.astype(jnp.bfloat16)
    grad_up = jnp.einsum("td,tf->df", rows2, grad_pre_low, preferred_element_type=jnp.float32)
    grad_norm2 = back_columns(
        jnp.einsum("tf,df->td", grad_pre_low, up_full, preferred_element_type=jnp.float32)
    )
    grad_hidden1 = grad_given + norm_backward(grad_norm2, normed2, inverse2, ln2_gain)
    branch_low = grad_hidden1.astype(jnp.bfloat16)
    grad_branch = lax.all_gather(branch_low, "col", axis=1, tiled=True)
    grad_outw = jnp.einsum("tc,td->cd", attn_low, grad_branch, preferred_element_type=jnp.float32)
    grad_attn = jnp.einsum(
        "td,cd->tc", grad_branch, out_full, preferred_element_type=jnp.float32
    ).astype(jnp.bfloat16)
    grad_attn = grad_attn.reshape(slots, span, heads_here, HEAD)
    grad_query, grad_keys, grad_values = lax.map(
        partial(backward_slot, slopes), (query, keys, values, grad_attn, lse, lengths)
    )
    stacked = jnp.stack((grad_query, grad_keys, grad_values), axis=3).reshape(
        rows, 3 * heads_here * HEAD
    )
    stacked_low = stacked.astype(jnp.bfloat16)
    grad_qkv = jnp.einsum("td,tc->dc", rows1, stacked_low, preferred_element_type=jnp.float32)
    grad_norm1 = back_columns(
        jnp.einsum("tc,dc->td", stacked_low, qkv_full, preferred_element_type=jnp.float32)
    )
    grad_input = grad_hidden1 + norm_backward(grad_norm1, normed1, inverse1, ln1_gain)
    small = lax.psum(
        (
            jnp.sum(grad_norm1 * normed1, axis=0),
            jnp.sum(grad_norm1, axis=0),
            jnp.sum(grad_query.reshape(rows, heads_here * HEAD), axis=0),
            jnp.sum(grad_values.reshape(rows, heads_here * HEAD), axis=0),
            jnp.sum(grad_hidden1, axis=0),
            jnp.sum(grad_norm2 * normed2, axis=0),
            jnp.sum(grad_norm2, axis=0),
            jnp.sum(grad_pre, axis=0),
            jnp.sum(grad_given, axis=0),
        ),
        ("dp", "row"),
    )
    local = (grad_qkv, grad_up, grad_outw, grad_down)
    whole = (
        lax.psum(local[0].astype(jnp.bfloat16), "dp").astype(jnp.float32),
        lax.psum(local[1].astype(jnp.bfloat16), "dp").astype(jnp.float32),
        lax.psum(local[2].astype(jnp.bfloat16), "dp").astype(jnp.float32),
        lax.psum(local[3].astype(jnp.bfloat16), "dp").astype(jnp.float32),
    )
    summed = (
        lax.psum_scatter(
            whole[0].astype(jnp.bfloat16), "row", scatter_dimension=0, tiled=True
        ).astype(jnp.float32),
        lax.psum_scatter(
            whole[1].astype(jnp.bfloat16), "row", scatter_dimension=0, tiled=True
        ).astype(jnp.float32),
        lax.psum_scatter(
            whole[2].astype(jnp.bfloat16), "row", scatter_dimension=1, tiled=True
        ).astype(jnp.float32),
        lax.psum_scatter(
            whole[3].astype(jnp.bfloat16), "row", scatter_dimension=1, tiled=True
        ).astype(jnp.float32),
    )
    return (
        jnp.transpose(result),
        jnp.transpose(grad_input),
        small[0],
        small[1],
        summed[0],
        small[2],
        small[3],
        summed[2],
        small[4],
        small[5],
        small[6],
        summed[1],
        small[7],
        summed[3],
        small[8],
    )


def solution(mesh):
    return jax.shard_map(
        body,
        mesh=mesh,
        in_specs=(
            P("col", ("dp", "row")),
            P(("dp", "row")),
            P("col"),
            P("col"),
            P("row", "col"),
            P("col"),
            P("col"),
            P("col", "row"),
            P("col"),
            P("col"),
            P("col"),
            P("row", "col"),
            P("col"),
            P("col", "row"),
            P("col"),
            P("col", ("dp", "row")),
        ),
        out_specs=(
            P("col", ("dp", "row")),
            P("col", ("dp", "row")),
            P("col"),
            P("col"),
            P("row", "col"),
            P("col"),
            P("col"),
            P("col", "row"),
            P("col"),
            P("col"),
            P("col"),
            P("row", "col"),
            P("col"),
            P("col", "row"),
            P("col"),
        ),
        check_vma=False,
    )
```

profile of v0, /device:TPU:0, one launch (start us, length us, event | category | flops | bytes accessed | tf_op | source)
XLA Modules:
  0.0 1329.2 jit_solution(10266186835196599832)
XLA Ops:
  34.8 53.8 %all-gather.9.cloned.1.call-done = bf16[2048,1024]{1,0:T(8,128)(2,1)} async-done(((bf16[2048,512]{1,0:T(8,128)(2,1)}), bf16[2048,1024]{1,0:T(8,128)(2,1)}) %all-gather.9.cloned.1.call-update) | async-done | bytes 4194320 | tf_op jit(solution)/shard_map/all_gather | solution.py:31
  88.6 65.1 %all-gather.11.cloned.1.call-done = bf16[1024,1536]{1,0:T(8,128)(2,1)} async-done(((bf16[256,1536]{1,0:T(8,128)(2,1)}), bf16[1024,1536]{1,0:T(8,128)(2,1)}) %all-gather.11.cloned.1.call-update) | async-done | bytes 3145744 | tf_op jit(solution)/shard_map/all_gather | solution.py:109
  153.7 9.8 fusion.100
  198.4 53.5 %while.30 = (s32[]{:T(128)}, bf16[4,512,8,64]{1,3,2,0:T(8,128)(2,1)}, f32[4,8,512]{2,1,0:T(8,128)}, bf16[4,512,8,64]{1,3,2,0:T(8,128)(2,1)}, s32[4]{0:T(128)S(1)...) while((s32[]{:T(128)}, ...), condition=%wide.region_7.8_spmd.clone.clone, body=%wide.region_4.7_spmd.clone.sunk.clone | while | flops 575664640 | bytes 49942764 | solution.py:130
  266.0 97.4 %reduce-scatter.9.cloned.1.call-done = f32[2048,512]{1,0:T(8,128)} async-done(((f32[2048,1024]{1,0:T(8,128)}), f32[2048,512]{1,0:T(8,128)}) %reduce-scatter.9.cloned.1.call-update) | async-done | bytes 4194320 | tf_op jit(solution)/shard_map/reduce_scatter | solution.py:132
  390.2 55.4 %all-gather.17.cloned.1.call-done = bf16[1024,2048]{1,0:T(8,128)(2,1)} async-done(((bf16[256,2048]{1,0:T(8,128)(2,1)}), bf16[1024,2048]{1,0:T(8,128)(2,1)}) %all-gather.17.cloned.1.call-update) | async-done | bytes 4194320 | tf_op jit(solution)/shard_map/all_gather | solution.py:110
  445.6 56.8 %all-gather.15.cloned.1.call-done = bf16[2048,1024]{1,0:T(8,128)(2,1)} async-done(((bf16[2048,512]{1,0:T(8,128)(2,1)}), bf16[2048,1024]{1,0:T(8,128)(2,1)}) %all-gather.15.cloned.1.call-update) | async-done | bytes 4194320 | tf_op jit(solution)/shard_map/all_gather | solution.py:31
  502.4 15.3 %fusion.102 = f32[2048,2048]{1,0:T(8,128)} fusion(bf16[2048,1024]{1,0:T(8,128)(2,1)} %all-gather.15.cloned.1.call-done, bf16[1024,2048]{1,0:T(8,128)(2,1)} %all-gather.17.cloned.1.call-done), kind=kOutput, calls=%fused_computation.144 | convolution fusion | flops 8589934592 | bytes 25165824 | tf_op jit(solution)/shard_map/dot_general | solution.py:141
  517.7 43.1 %all-gather.21.cloned.1.call-done = bf16[2048,1024]{1,0:T(8,128)(2,1)} async-done(((bf16[2048,512]{1,0:T(8,128)(2,1)}), bf16[2048,1024]{1,0:T(8,128)(2,1)}) %all-gather.21.cloned.1.call-update) | async-done | bytes 4194320 | tf_op jit(solution)/shard_map/all_gather | solution.py:153
  560.8 82.2 %all-gather.19.cloned.1.call-done = bf16[2048,1024]{1,0:T(8,128)(2,1)} async-done(((bf16[2048,256]{1,0:T(8,128)(2,1)}), bf16[2048,1024]{1,0:T(8,128)(2,1)}) %all-gather.19.cloned.1.call-update) | async-done | bytes 4194320 | tf_op jit(solution)/shard_map/all_gather | solution.py:112
  643.0 27.5 %fusion.91 = (f32[2048]{0:T(1024)}, bf16[2048,2048]{1,0:T(8,128)(2,1)}, bf16[2048,2048]{1,0:T(8,128)(2,1)}) fusion(f32[2048,2048]{1,0:T(8,128)} %fusion.102, f32[2048]{0:T(1024)S(1)} %copy-done.34, bf16[2048,1024]{1,0:T(8,128)(2,1)} %all-gather.21.cloned.1.call-done, bf16[2048,1024]{1,0:T(8,128)(2,1)} %all-gather.19.cloned.1.call-done), kind=kOutput, calls=%fused_computation.136 | convolution fusion | flops 8690595840 | bytes 41959424 | tf_op jit(solution)/shard_map/td,fd->tf/dot_general | solution.py:155
  670.5 13.0 fusion.84
  683.6 13.8 %convolution_convert_fusion.2 = bf16[2048,1024]{1,0:T(8,128)(2,1)} fusion(bf16[2048,2048]{1,0:T(8,128)(2,1)} %get-tuple-element.304, bf16[2048,1024]{1,0:T(8,128)(2,1)} %all-gather.19.cloned.1.call-done), kind=kOutput, calls=%fused_computation.122 | convolution fusion | flops 8592031744 | bytes 16777216 | tf_op jit(solution)/shard_map/dot_general | solution.py:144
  697.4 38.7 %reduce-scatter.13.cloned.1.call-done = bf16[2048,512]{1,0:T(8,128)(2,1)} async-done(((bf16[2048,1024]{1,0:T(8,128)(2,1)}), bf16[2048,512]{1,0:T(8,128)(2,1)}) %reduce-scatter.13.cloned.1.call-update) | async-done | bytes 2097168 | tf_op jit(solution)/shard_map/reduce_scatter | solution.py:35
  747.9 44.8 %reduce-scatter.11.cloned.1.call-done = bf16[2048,512]{1,0:T(8,128)(2,1)} async-done(((bf16[2048,1024]{1,0:T(8,128)(2,1)}), bf16[2048,512]{1,0:T(8,128)(2,1)}) %reduce-scatter.11.cloned.1.call-update) | async-done | bytes 2097168 | tf_op jit(solution)/shard_map/reduce_scatter | solution.py:147
  804.6 14.2 %convolution_convert_fusion.3 = bf16[2048,1024]{1,0:T(8,128)(2,1)} fusion(bf16[2048,2048]{1,0:T(8,128)(2,1)} %get-tuple-element.304, bf16[2048,1024]{1,0:T(8,128)(2,1)} %all-gather.21.cloned.1.call-done), kind=kOutput, calls=%fused_computation.123 | convolution fusion | flops 8592031744 | bytes 16777216 | tf_op jit(solution)/shard_map/tf,td->fd/dot_general | solution.py:154
  818.8 14.1 %fusion.87 = bf16[1024,2048]{1,0:T(8,128)(2,1)} fusion(bf16[2048,1024]{1,0:T(8,128)(2,1)} %all-gather.15.cloned.1.call-done, bf16[2048,2048]{1,0:T(8,128)(2,1)} %get-tuple-element.296), kind=kOutput, calls=%fused_computation.121 | convolution fusion | flops 8592031744 | bytes 16777216 | tf_op jit(solution)/shard_map/td,tf->df/dot_general | solution.py:158
  833.0 28.5 %all-gather.23.cloned.1.call-done = bf16[2048,1024]{1,0:T(8,128)(2,1)} async-done(((bf16[2048,512]{1,0:T(8,128)(2,1)}), bf16[2048,1024]{1,0:T(8,128)(2,1)}) %all-gather.23.cloned.1.call-update) | async-done | bytes 4194320 | tf_op jit(solution)/shard_map/all_gather | solution.py:164
  880.7 133.4 %while.31 = (s32[]{:T(128)}, f32[4,512,8,64]{1,3,2,0:T(8,128)}, bf16[4,512,8,64]{1,3,2,0:T(8,128)(2,1)}, f32[4,512,8,64]{1,3,2,0:T(8,128)}, bf16[4,512,8,64]{1,3...) while((s32[]{:T(128)}, f32[4,512,8,64]{1,3,2,0:T(8,128)}, ...), condition=%wide.region_21.22_spmd.clone.clone, body=%wide.region_19.21_spmd.clone.sunk.clone | while | flops 1366815232 | bytes 122771752 | solution.py:170
  1050.7 61.7 %reduce-scatter.17.cloned.1.call-done = bf16[256,1536]{1,0:T(8,128)(2,1)} async-done(((bf16[1024,1536]{1,0:T(8,128)(2,1)}), bf16[256,1536]{1,0:T(8,128)(2,1)}) %reduce-scatter.17.cloned.1.call-update) | async-done | bytes 786448 | tf_op jit(solution)/shard_map/reduce_scatter | solution.py:204
  1112.4 11.7 convolution_convert_fusion.1
  1132.2 51.7 %all-reduce.8.cloned.1.call-done = (bf16[256,1536]{1,0:T(8,128)(2,1)}, bf16[512,256]{1,0:T(8,128)(2,1)}, bf16[256,2048]{1,0:T(8,128)(2,1)}, bf16[2048,256]{1,0:T(8,128)(2,1)}) async-done(((bf16[256,1536]{1,0:T(8,128)(2,1)}, bf16[512,256]{1,0:T(8,128)(2,1)}, bf16[256,2048]{1,0:T(8,128)(2,1)}, bf16[2048,256]{1,0:T(8,128)(2,1)}), (bf16[256,1536]{1,0:T(8,128)(2,1)}, bf16[512,256]{1,0:T(8,128)(2,1)}, ...) | async-done | bytes 3145744 | tf_op jit(solution)/shard_map/psum | solution.py:198
  1192.5 47.9 %reduce-scatter.15.cloned.1.call-done = bf16[2048,512]{1,0:T(8,128)(2,1)} async-done(((bf16[2048,1024]{1,0:T(8,128)(2,1)}), bf16[2048,512]{1,0:T(8,128)(2,1)}) %reduce-scatter.15.cloned.1.call-update) | async-done | bytes 2097168 | tf_op jit(solution)/shard_map/reduce_scatter | solution.py:35
  1262.6 59.9 %all-reduce = (f32[512]{0:T(512)}, f32[512]{0:T(512)}, f32[512]{0:T(512)}, f32[512]{0:T(512)}, f32[512]{0:T(512)}, /*index=5*/f32[512]{0:T(512)}, f32[512]{0:T(512)}, f32[2048]{0:T(1024)}, f32[512]{0:T(512)}) all-reduce(f32[512]{0:T(512)S(1)} %get-tuple-element.228, ...), channel_id=1, replica_groups=mesh['dp'=4,'row'=4,'col'=2] {'dp','row'}, use_global_device_ids=true, to_apply=%region_28.29 | all-reduce | flops 6144 | bytes 49152 | tf_op jit(solution)/shard_map/psum | solution.py:182
  (286 shorter events, 407.8 us)
Async XLA Ops:
  7.2 81.4 %all-gather.9.cloned.1.call-start = ((), (), s32[]{:S(2)}) async-start(), calls=%async_computation.8 | async-start | bytes 6291456 | tf_op jit(solution)/shard_map/all_gather | solution.py:31
  31.4 122.2 %all-gather.11.cloned.1.call-start = ((), (), s32[]{:S(2)}) async-start(), calls=%async_computation.9 | async-start | bytes 3932160 | tf_op jit(solution)/shard_map/all_gather | solution.py:109
  32.2 225.6 %all-gather.13.cloned.1.call-start = ((), (), s32[]{:S(2)}) async-start(), calls=%async_computation.10 | async-start | bytes 1310720 | tf_op jit(solution)/shard_map/all_gather | solution.py:111
  32.9 330.4 %reduce-scatter.9.cloned.1.call-start = ((), (), s32[]{:S(2)}) async-start(), calls=%async_computation.11 | async-start | bytes 12582912 | tf_op jit(solution)/shard_map/reduce_scatter | solution.py:132
  33.2 130.3 %copy-start.3 = (bf16[4,512,8,64]{1,3,2,0:T(8,128)(2,1)}, bf16[4,512,8,64]{1,3,2,0:T(8,128)(2,1)S(1)}, u32[]{:S(2)}) copy-start(bf16[4,512,8,64]{1,3,2,0:T(8,128)(2,1)S(1)} %fusion.99) | copy-start | bytes 6291460
  265.3 98.1 %copy-start.30 = (f32[512]{0:T(512)S(1)}, f32[512]{0:T(512)}, u32[]{:S(2)}) copy-start(f32[512]{0:T(512)} %param.28) | copy-start | bytes 6148
  265.3 180.3 %all-gather.17.cloned.1.call-start = ((), (), s32[]{:S(2)}) async-start(), calls=%async_computation.13 | async-start | bytes 5242880 | tf_op jit(solution)/shard_map/all_gather | solution.py:110
  265.9 110.3 %copy-start.18 = (f32[512]{0:T(512)S(1)}, f32[512]{0:T(512)}, u32[]{:S(2)}) copy-start(f32[512]{0:T(512)} %param.29) | copy-start | bytes 6148
  265.9 110.3 %copy-start.26 = (f32[512]{0:T(512)S(1)}, f32[512]{0:T(512)}, u32[]{:S(2)}) copy-start(f32[512]{0:T(512)} %param.30) | copy-start | bytes 6148
  265.9 236.5 %all-gather.15.cloned.1.call-start = ((), (), s32[]{:S(2)}) async-start(), calls=%async_computation.12 | async-start | bytes 6291456 | tf_op jit(solution)/shard_map/all_gather | solution.py:31
  379.9 180.9 %all-gather.21.cloned.1.call-start = ((), (), s32[]{:S(2)}) async-start(), calls=%async_computation.16 | async-start | bytes 6291456 | tf_op jit(solution)/shard_map/all_gather | solution.py:153
  389.4 253.6 %all-gather.19.cloned.1.call-start = ((), (), s32[]{:S(2)}) async-start(), calls=%async_computation.14 | async-start | bytes 5242880 | tf_op jit(solution)/shard_map/all_gather | solution.py:112
  390.2 252.9 %copy-start.34 = (f32[2048]{0:T(1024)S(1)}, f32[2048]{0:T(1024)}, u32[]{:S(2)}) copy-start(f32[2048]{0:T(1024)} %param.32) | copy-start | bytes 24580
  390.2 346.0 %reduce-scatter.13.cloned.1.call-start = ((), (), s32[]{:S(2)}) async-start(), calls=%async_computation.17 | async-start | bytes 6291456 | tf_op jit(solution)/shard_map/reduce_scatter | solution.py:35
  683.5 109.2 %reduce-scatter.11.cloned.1.call-start = ((), (), s32[]{:S(2)}) async-start(), calls=%async_computation.15 | async-start | bytes 6291456 | tf_op jit(solution)/shard_map/reduce_scatter | solution.py:147
  697.4 95.4 %copy-start.27 = (f32[512]{0:T(512)S(1)}, f32[512]{0:T(512)}, u32[]{:S(2)}) copy-start(f32[512]{0:T(512)} %param.34) | copy-start | bytes 6148
  697.4 164.1 %all-gather.23.cloned.1.call-start = ((), (), s32[]{:S(2)}) async-start(), calls=%async_computation.18 | async-start | bytes 6291456 | tf_op jit(solution)/shard_map/all_gather | solution.py:164
  736.2 56.6 %copy-start.7 = (bf16[2048,512]{1,0:T(8,128)(2,1)S(1)}, bf16[2048,512]{1,0:T(8,128)(2,1)}, u32[]{:S(2)}) copy-start(bf16[2048,512]{1,0:T(8,128)(2,1)} %reduce-scatter.13.cloned.1.call-done) | copy-start | bytes 6291460
  804.5 242.9 %reduce-scatter.23.cloned.1.call-start = ((), (), s32[]{:S(2)}) async-start(), calls=%async_computation.23 | async-start | bytes 5242880 | tf_op jit(solution)/shard_map/reduce_scatter | solution.py:213
  818.8 228.7 %reduce-scatter.21.cloned.1.call-start = ((), (), s32[]{:S(2)}) async-start(), calls=%async_computation.22 | async-start | bytes 5242880 | tf_op jit(solution)/shard_map/reduce_scatter | solution.py:207
  832.9 217.7 %reduce-scatter.19.cloned.1.call-start = ((), (), s32[]{:S(2)}) async-start(), calls=%async_computation.21 | async-start | bytes 1310720 | tf_op jit(solution)/shard_map/reduce_scatter | solution.py:210
  1014.1 98.2 %reduce-scatter.17.cloned.1.call-start = ((), (), s32[]{:S(2)}) async-start(), calls=%async_computation.20 | async-start | bytes 3932160 | tf_op jit(solution)/shard_map/reduce_scatter | solution.py:204
  1047.4 136.4 %all-reduce.8.cloned.1.call-start = ((), (), s32[]{:S(2)}) async-start(), calls=%async_computation.24 | async-start | bytes 6291456 | tf_op jit(solution)/shard_map/psum | solution.py:198
  1112.4 128.0 %reduce-scatter.15.cloned.1.call-start = ((), (), s32[]{:S(2)}) async-start(), calls=%async_computation.19 | async-start | bytes 6291456 | tf_op jit(solution)/shard_map/reduce_scatter | solution.py:35
  (45 other events, 427.9 us)
Sparse Core Ops, SparseCore 0:
  31.5 56.9 all-gather.8
  90.1 63.4 all-gather.10
  155.2 28.8 all-gather.12
  265.4 97.8 reduce-scatter.8
  364.8 80.7 all-gather.16
  447.1 55.2 all-gather.14
  504.0 56.7 all-gather.20
  562.4 80.5 all-gather.18
  683.6 52.4 reduce-scatter.12
  738.3 54.3 reduce-scatter.10
  804.7 56.8 all-gather.22
  863.8 76.7 reduce-scatter.22
  942.8 77.3 reduce-scatter.20
  1023.0 27.6 reduce-scatter.18
  1053.4 58.8 reduce-scatter.16
  1114.8 68.9 all-reduce.7
  1186.0 54.3 reduce-scatter.14
where the time goes:
time: 1340 us; the launch traced here: 1330 us
  waiting for transfers between devices  733 us (55%)
  matrix products  269 us (20%)
  other arithmetic  124 us (9%)
  local copies, waits for them, and re-layouts  96.6 us (7%)
  blocking collectives  90.2 us (7%)
  between operations  14.5 us (1%)
    all_gather x2, waiting for transfers between devices, gather_rows(): return lax.all_gather(value, 'col', axis=1, tiled=True)  111 us
    reduce_scatter x1, waiting for transfers between devices, body(): lax.psum_scatter(jnp.dot(attn_low, out_full, preferred_element_type=jnp.f...  97.4 us
    reduce_scatter x2, waiting for transfers between devices, back_columns(): lax.psum_scatter(value.astype(jnp.bfloat16), 'col', scatter_dimension=1,...  86.7 us
    all_gather x1, waiting for transfers between devices, body(): lax.all_gather(w_down, 'row', axis=1, tiled=True)  82.2 us
    all_gather x1, waiting for transfers between devices, body(): lax.all_gather(w_qkv, 'row', axis=0, tiled=True)  65.1 us
    reduce_scatter x1, waiting for transfers between devices, body(): lax.psum_scatter(whole[0].astype(jnp.bfloat16), 'row', scatter_dimension=...  61.7 us
    psum x1, blocking collectives, body(): lax.psum((jnp.sum(grad_norm1 * normed1, axis=0), jnp.sum(grad_norm1, axis...  59.9 us
    all_gather x1, waiting for transfers between devices, body(): lax.all_gather(w_up, 'row', axis=0, tiled=True)  55.4 us
  transfers between devices with their start and end apart: 17, of which 14 were waited for; matrix products, arithmetic and copies ran while one was open for 30% of the time, Pallas kernels for 0%

commit v1 on v0

--- a/solution.py
+++ b/solution.py
@@ -8,6 +8,27 @@
 HEAD = 64
 EPS = 1e-05
 NEG = -1e30
+
+
+def laid_out(tiles, dim):
+    shape = list(tiles.shape[1:])
+    shape[dim] *= tiles.shape[0]
+    return jnp.moveaxis(tiles, 0, dim).reshape(shape)
+
+
+def grow_blocks(shard, axis):
+    peers, index = (lax.axis_size(axis), lax.axis_index(axis))
+    blocks, distance = (shard[None], 1)
+    while distance < peers:
+        other = lax.ppermute(blocks, axis, [(i, i ^ distance) for i in range(peers)])
+        low = index & distance == 0
+        blocks = jnp.concatenate([jnp.where(low, blocks, other), jnp.where(low, other, blocks)])
+        distance *= 2
+    return blocks
+
+
+def collect(x, axis, dim):
+    return laid_out(grow_blocks(x, axis), dim)
 
 
 def norm_forward(value, gain, shift):
@@ -109,7 +130,7 @@
         lax.all_gather(w_qkv, "row", axis=0, tiled=True),
         lax.all_gather(w_up, "row", axis=0, tiled=True),
         lax.all_gather(w_out, "row", axis=1, tiled=True),
-        lax.all_gather(w_down, "row", axis=1, tiled=True),
+        collect(w_down, "row", 1),
     )
     normed1, inverse1, low1 = norm_forward(tokens_in, ln1_gain, ln1_shift)
     rows1 = gather_rows(low1)

time: 1340 us -> 1280 us (0.955)
  waiting for transfers between devices: 733 us -> 656 us
    ppermute x0 -> x2, waiting for transfers between devices: none -> 160 us  [grow_blocks(): lax.ppermute(blocks, axis, [(i, i ^ distance) for i in range(peers)])]
    all_gather x1 -> x0, waiting for transfers between devices: 82.2 us -> none  [body(): lax.all_gather(w_down, 'row', axis=1, tiled=True)]
    all_gather x2, waiting for transfers between devices: 111 us -> 53.8 us  [gather_rows(): return lax.all_gather(value, 'col', axis=1, tiled=True)]
    all_gather x1, waiting for transfers between devices: 55.4 us -> 0.01 us  [body(): lax.all_gather(w_up, 'row', axis=0, tiled=True)]
    all_gather x1, waiting for transfers between devices: 43.1 us -> 0.01 us  [body(): grad_full = lax.all_gather(grad_low, 'col', axis=1, tiled=True)]
    dot_general x1, matrix products: 15.3 us -> 29.2 us  [body(): pre = jnp.dot(rows2, up_full, preferred_element_type=jnp.float32) + bias_up]
    unnamed x76 -> x81, local copies, waits for them, and re-layouts: 47.8 us -> 51.5 us
  transfers between devices with their start and end apart: 17 -> 18, of which waited for: 14 -> 12; matrix products, arithmetic and copies ran while one was open for 30% -> 33% of each run, Pallas kernels for 0% -> 0%
where the time goes in v1:
time: 1280 us; the launch traced here: 1270 us
  waiting for transfers between devices  656 us (51%)
  matrix products  278 us (22%)
  other arithmetic  131 us (10%)
  local copies, waits for them, and re-layouts  100 us (8%)
  blocking collectives  90.2 us (7%)
  between operations  14.8 us (1%)
    ppermute x2, waiting for transfers between devices, grow_blocks(): lax.ppermute(blocks, axis, [(i, i ^ distance) for i in range(peers)])  160 us
    reduce_scatter x1, waiting for transfers between devices, body(): lax.psum_scatter(jnp.dot(attn_low, out_full, preferred_element_type=jnp.f...  97.4 us
    reduce_scatter x2, waiting for transfers between devices, back_columns(): lax.psum_scatter(value.astype(jnp.bfloat16), 'col', scatter_dimension=1,...  87.6 us
    all_gather x1, waiting for transfers between devices, body(): lax.all_gather(w_qkv, 'row', axis=0, tiled=True)  65.1 us
    reduce_scatter x1, waiting for transfers between devices, body(): lax.psum_scatter(whole[0].astype(jnp.bfloat16), 'row', scatter_dimension=...  61.7 us
    psum x1, blocking collectives, body(): lax.psum((jnp.sum(grad_norm1 * normed1, axis=0), jnp.sum(grad_norm1, axis...  59.9 us
    all_gather x2, waiting for transfers between devices, gather_rows(): return lax.all_gather(value, 'col', axis=1, tiled=True)  53.8 us
    psum x1, waiting for transfers between devices, body(): lax.psum(local[0].astype(jnp.bfloat16), 'dp').astype(jnp.float32)  51.6 us
  transfers between devices with their start and end apart: 18, of which 12 were waited for; matrix products, arithmetic and copies ran while one was open for 33% of the time, Pallas kernels for 0%

profile of v1, /device:TPU:0, one launch (start us, length us, event | category | flops | bytes accessed | tf_op | source)
XLA Modules:
  0.0 1274.0 jit_solution(15654692455420734214)
XLA Ops:
  17.6 9.6 all-reduce.4
  34.8 53.8 %all-gather.8.cloned.1.call-done = bf16[2048,1024]{1,0:T(8,128)(2,1)} async-done(((bf16[2048,512]{1,0:T(8,128)(2,1)}), bf16[2048,1024]{1,0:T(8,128)(2,1)}) %all-gather.8.cloned.1.call-update) | async-done | bytes 4194320 | tf_op jit(solution)/shard_map/all_gather | solution.py:52
  88.6 65.1 %all-gather.10.cloned.1.call-done = bf16[1024,1536]{1,0:T(8,128)(2,1)} async-done(((bf16[256,1536]{1,0:T(8,128)(2,1)}), bf16[1024,1536]{1,0:T(8,128)(2,1)}) %all-gather.10.cloned.1.call-update) | async-done | bytes 3145744 | tf_op jit(solution)/shard_map/all_gather | solution.py:130
  153.7 9.8 fusion.102
  198.4 53.6 %while.30 = (s32[]{:T(128)}, bf16[4,512,8,64]{1,3,2,0:T(8,128)(2,1)}, f32[4,8,512]{2,1,0:T(8,128)}, bf16[4,512,8,64]{1,3,2,0:T(8,128)(2,1)}, s32[4]{0:T(128)S(1)...) while((s32[]{:T(128)}, ...), condition=%wide.region_7.8_spmd.clone.clone, body=%wide.region_4.7_spmd.clone.sunk.clone | while | flops 575664640 | bytes 49942764 | solution.py:151
  266.0 97.4 %reduce-scatter.9.cloned.1.call-done = f32[2048,512]{1,0:T(8,128)} async-done(((f32[2048,1024]{1,0:T(8,128)}), f32[2048,512]{1,0:T(8,128)}) %reduce-scatter.9.cloned.1.call-update) | async-done | bytes 4194320 | tf_op jit(solution)/shard_map/reduce_scatter | solution.py:153
  382.5 77.0 %collective-permute-done = bf16[1,2048,256]{1,2,0:T(8,128)(2,1)} collective-permute-done((bf16[1,2048,256]{1,2,0:T(8,128)(2,1)S(1)}, bf16[1,2048,256]{1,2,0:T(8,128)(2,1)}, u32[]{:S(2)}, u32[]{:S(2)}) %collective-permute-start) | collective-permute-done | bytes 1048608 | tf_op jit(solution)/shard_map/ppermute | solution.py:23
  472.0 83.2 %collective-permute-done.1 = bf16[2,2048,256]{1,2,0:T(8,128)(2,1)} collective-permute-done((bf16[2,2048,256]{1,2,0:T(8,128)(2,1)}, bf16[2,2048,256]{1,2,0:T(8,128)(2,1)}, u32[]{:S(2)}, u32[]{:S(2)}) %collective-permute-start.1) | collective-permute-done | bytes 2097184 | tf_op jit(solution)/shard_map/ppermute | solution.py:23
  559.5 29.2 %multiply_convert_fusion.1 = (bf16[2048,2048]{1,0:T(8,128)(2,1)}, f32[2048,2048]{1,0:T(8,128)}) fusion(f32[2048]{0:T(1024)S(1)} %copy-done.35, bf16[2048,1024]{1,0:T(8,128)(2,1)} %all-gather.14.cloned.1.call-done, bf16[1024,2048]{1,0:T(8,128)(2,1)} %all-gather.16.cloned.1.call-done), kind=kOutput, calls=%fused_computation.79 | convolution fusion | flops 8631877632 | bytes 33562624 | tf_op jit(solution)/shard_map/dot_general | solution.py:162
  588.7 24.0 %fusion.101 = (f32[2048]{0:T(1024)}, bf16[2048,2048]{1,0:T(8,128)(2,1)S(1)}) fusion(f32[2048,2048]{1,0:T(8,128)} %get-tuple-element.320, f32[2048]{0:T(1024)S(1)} %copy-done.35, bf16[2048,1024]{1,0:T(8,128)(2,1)} %all-gather.18.cloned.1.call-done, bf16[2048,1024]{0,1:T(8,128)(2,1)} %bitcast.239), kind=kOutput, calls=%fused_computation.152 | convolution fusion | flops 8682207232 | bytes 33570816 | tf_op jit(solution)/shard_map/td,fd->tf/dot_general | solution.py:176
  615.9 10.7 fusion.87
  626.8 13.9 %convolution_convert_fusion.2 = bf16[2048,1024]{1,0:T(8,128)(2,1)} fusion(bf16[2048,2048]{1,0:T(8,128)(2,1)} %get-tuple-element.319, bf16[2048,1024]{0,1:T(8,128)(2,1)} %bitcast.240), kind=kOutput, calls=%fused_computation.128 | convolution fusion | flops 8592031744 | bytes 16777216 | tf_op jit(solution)/shard_map/dot_general | solution.py:165
  640.7 39.7 %reduce-scatter.13.cloned.1.call-done = bf16[2048,512]{1,0:T(8,128)(2,1)} async-done(((bf16[2048,1024]{1,0:T(8,128)(2,1)}), bf16[2048,512]{1,0:T(8,128)(2,1)}) %reduce-scatter.13.cloned.1.call-update) | async-done | bytes 2097168 | tf_op jit(solution)/shard_map/reduce_scatter | solution.py:56
  692.2 45.0 %reduce-scatter.11.cloned.1.call-done = bf16[2048,512]{1,0:T(8,128)(2,1)} async-done(((bf16[2048,1024]{1,0:T(8,128)(2,1)}), bf16[2048,512]{1,0:T(8,128)(2,1)}) %reduce-scatter.11.cloned.1.call-update) | async-done | bytes 2097168 | tf_op jit(solution)/shard_map/reduce_scatter | solution.py:168
  748.9 14.5 %convolution_convert_fusion.3 = bf16[2048,1024]{1,0:T(8,128)(2,1)} fusion(bf16[2048,2048]{1,0:T(8,128)(2,1)} %get-tuple-element.319, bf16[2048,1024]{1,0:T(8,128)(2,1)} %all-gather.18.cloned.1.call-done), kind=kOutput, calls=%fused_computation.129 | convolution fusion | flops 8592031744 | bytes 16777216 | tf_op jit(solution)/shard_map/tf,td->fd/dot_general | solution.py:175
  763.5 14.0 %fusion.90 = bf16[1024,2048]{1,0:T(8,128)(2,1)} fusion(bf16[2048,1024]{1,0:T(8,128)(2,1)} %all-gather.14.cloned.1.call-done, bf16[2048,2048]{1,0:T(8,128)(2,1)} %copy-done.38), kind=kOutput, calls=%fused_computation.127 | convolution fusion | flops 8592031744 | bytes 16777216 | tf_op jit(solution)/shard_map/td,tf->df/dot_general | solution.py:179
  777.6 28.3 %all-gather.20.cloned.1.call-done = bf16[2048,1024]{1,0:T(8,128)(2,1)} async-done(((bf16[2048,512]{1,0:T(8,128)(2,1)}), bf16[2048,1024]{1,0:T(8,128)(2,1)}) %all-gather.20.cloned.1.call-update) | async-done | bytes 4194320 | tf_op jit(solution)/shard_map/all_gather | solution.py:185
  825.1 133.3 %while.31 = (s32[]{:T(128)}, f32[4,512,8,64]{1,3,2,0:T(8,128)}, bf16[4,512,8,64]{1,3,2,0:T(8,128)(2,1)}, f32[4,512,8,64]{1,3,2,0:T(8,128)}, bf16[4,512,8,64]{1,3...) while((s32[]{:T(128)}, f32[4,512,8,64]{1,3,2,0:T(8,128)}, ...), condition=%wide.region_21.22_spmd.clone.clone, body=%wide.region_19.21_spmd.clone.sunk.clone | while | flops 1366815232 | bytes 122771752 | solution.py:191
  929.7 8.9 multiply_reduce_fusion.4
  995.2 61.7 %reduce-scatter.17.cloned.1.call-done = bf16[256,1536]{1,0:T(8,128)(2,1)} async-done(((bf16[1024,1536]{1,0:T(8,128)(2,1)}), bf16[256,1536]{1,0:T(8,128)(2,1)}) %reduce-scatter.17.cloned.1.call-update) | async-done | bytes 786448 | tf_op jit(solution)/shard_map/reduce_scatter | solution.py:225
  1056.9 11.7 convolution_convert_fusion.1
  1076.7 51.6 %all-reduce.8.cloned.1.call-done = (bf16[256,1536]{1,0:T(8,128)(2,1)}, bf16[512,256]{1,0:T(8,128)(2,1)}, bf16[256,2048]{1,0:T(8,128)(2,1)}, bf16[2048,256]{1,0:T(8,128)(2,1)}) async-done(((bf16[256,1536]{1,0:T(8,128)(2,1)}, bf16[512,256]{1,0:T(8,128)(2,1)}, bf16[256,2048]{1,0:T(8,128)(2,1)}, bf16[2048,256]{1,0:T(8,128)(2,1)}), (bf16[256,1536]{1,0:T(8,128)(2,1)}, bf16[512,256]{1,0:T(8,128)(2,1)}, ...) | async-done | bytes 3145744 | tf_op jit(solution)/shard_map/psum | solution.py:219
  1137.0 47.9 %reduce-scatter.15.cloned.1.call-done = bf16[2048,512]{1,0:T(8,128)(2,1)} async-done(((bf16[2048,1024]{1,0:T(8,128)(2,1)}), bf16[2048,512]{1,0:T(8,128)(2,1)}) %reduce-scatter.15.cloned.1.call-update) | async-done | bytes 2097168 | tf_op jit(solution)/shard_map/reduce_scatter | solution.py:56
  1207.1 59.9 %all-reduce = (f32[512]{0:T(512)}, f32[512]{0:T(512)}, f32[512]{0:T(512)}, f32[512]{0:T(512)}, f32[512]{0:T(512)}, /*index=5*/f32[512]{0:T(512)}, f32[512]{0:T(512)}, f32[2048]{0:T(1024)}, f32[512]{0:T(512)}) all-reduce(f32[512]{0:T(512)S(1)} %get-tuple-element.228, ...), channel_id=1, replica_groups=mesh['dp'=4,'row'=4,'col'=2] {'dp','row'}, use_global_device_ids=true, to_apply=%region_28.29 | all-reduce | flops 6144 | bytes 49152 | tf_op jit(solution)/shard_map/psum | solution.py:203
  (296 shorter events, 401.6 us)
Async XLA Ops:
  7.2 81.4 %all-gather.8.cloned.1.call-start = ((), (), s32[]{:S(2)}) async-start(), calls=%async_computation.8 | async-start | bytes 6291456 | tf_op jit(solution)/shard_map/all_gather | solution.py:52
  31.4 122.2 %all-gather.10.cloned.1.call-start = ((), (), s32[]{:S(2)}) async-start(), calls=%async_computation.9 | async-start | bytes 3932160 | tf_op jit(solution)/shard_map/all_gather | solution.py:130
  32.2 225.7 %all-gather.12.cloned.1.call-start = ((), (), s32[]{:S(2)}) async-start(), calls=%async_computation.10 | async-start | bytes 1310720 | tf_op jit(solution)/shard_map/all_gather | solution.py:132
  32.9 330.5 %reduce-scatter.9.cloned.1.call-start = ((), (), s32[]{:S(2)}) async-start(), calls=%async_computation.11 | async-start | bytes 12582912 | tf_op jit(solution)/shard_map/reduce_scatter | solution.py:153
  33.2 130.3 %copy-start.3 = (bf16[4,512,8,64]{1,3,2,0:T(8,128)(2,1)}, bf16[4,512,8,64]{1,3,2,0:T(8,128)(2,1)S(1)}, u32[]{:S(2)}) copy-start(bf16[4,512,8,64]{1,3,2,0:T(8,128)(2,1)S(1)} %fusion.100) | copy-start | bytes 6291460
  265.3 98.1 %copy-start.31 = (f32[512]{0:T(512)S(1)}, f32[512]{0:T(512)}, u32[]{:S(2)}) copy-start(f32[512]{0:T(512)} %param.28) | copy-start | bytes 6148
  265.4 294.1 %all-gather.16.cloned.1.call-start = ((), (), s32[]{:S(2)}) async-start(), calls=%async_computation.13 | async-start | bytes 5242880 | tf_op jit(solution)/shard_map/all_gather | solution.py:131
  266.0 110.3 %copy-start.19 = (f32[512]{0:T(512)S(1)}, f32[512]{0:T(512)}, u32[]{:S(2)}) copy-start(f32[512]{0:T(512)} %param.29) | copy-start | bytes 6148
  266.0 110.3 %copy-start.27 = (f32[512]{0:T(512)S(1)}, f32[512]{0:T(512)}, u32[]{:S(2)}) copy-start(f32[512]{0:T(512)} %param.30) | copy-start | bytes 6148
  266.0 293.5 %all-gather.14.cloned.1.call-start = ((), (), s32[]{:S(2)}) async-start(), calls=%async_computation.12 | async-start | bytes 6291456 | tf_op jit(solution)/shard_map/all_gather | solution.py:52
  380.0 208.7 %all-gather.18.cloned.1.call-start = ((), (), s32[]{:S(2)}) async-start(), calls=%async_computation.15 | async-start | bytes 6291456 | tf_op jit(solution)/shard_map/all_gather | solution.py:174
  380.7 78.8 %collective-permute-start = (bf16[1,2048,256]{1,2,0:T(8,128)(2,1)S(1)}, bf16[1,2048,256]{1,2,0:T(8,128)(2,1)}, u32[]{:S(2)}, u32[]{:S(2)}) collective-permute-start(bf16[1,2048,256]{1,2,0:T(8,128)(2,1)S(1)} %bitcast.238), channel_id=1, source_target_pairs={{0,2},{2,0},{4,6},{6,4},{1,3},{3,1},{5,7},{7,5},{8,10},{10,8},{12,... | collective-permute-start | bytes 3145736 | tf_op jit(solution)/shard_map/ppermute | solution.py:23
  462.4 92.8 %collective-permute-start.1 = (bf16[2,2048,256]{1,2,0:T(8,128)(2,1)}, bf16[2,2048,256]{1,2,0:T(8,128)(2,1)}, u32[]{:S(2)}, u32[]{:S(2)}) collective-permute-start(bf16[2,2048,256]{1,2,0:T(8,128)(2,1)} %pad_maximum_fusion.2), channel_id=1, source_target_pairs={{0,4},{2,6},{4,0},{6,2},{1,5},{3,7},{5,1},{7,3},{8,12},{10,14},{12... | collective-permute-start | bytes 6291464 | tf_op jit(solution)/shard_map/ppermute | solution.py:23
  472.0 208.5 %reduce-scatter.13.cloned.1.call-start = ((), (), s32[]{:S(2)}) async-start(), calls=%async_computation.16 | async-start | bytes 6291456 | tf_op jit(solution)/shard_map/reduce_scatter | solution.py:56
  626.7 110.4 %reduce-scatter.11.cloned.1.call-start = ((), (), s32[]{:S(2)}) async-start(), calls=%async_computation.14 | async-start | bytes 6291456 | tf_op jit(solution)/shard_map/reduce_scatter | solution.py:168
  640.7 96.5 %copy-start.28 = (f32[512]{0:T(512)S(1)}, f32[512]{0:T(512)}, u32[]{:S(2)}) copy-start(f32[512]{0:T(512)} %param.34) | copy-start | bytes 6148
  640.7 165.2 %all-gather.20.cloned.1.call-start = ((), (), s32[]{:S(2)}) async-start(), calls=%async_computation.17 | async-start | bytes 6291456 | tf_op jit(solution)/shard_map/all_gather | solution.py:185
  680.4 56.7 %copy-start.7 = (bf16[2048,512]{1,0:T(8,128)(2,1)S(1)}, bf16[2048,512]{1,0:T(8,128)(2,1)}, u32[]{:S(2)}) copy-start(bf16[2048,512]{1,0:T(8,128)(2,1)} %reduce-scatter.13.cloned.1.call-done) | copy-start | bytes 6291460
  748.9 242.8 %reduce-scatter.23.cloned.1.call-start = ((), (), s32[]{:S(2)}) async-start(), calls=%async_computation.22 | async-start | bytes 5242880 | tf_op jit(solution)/shard_map/reduce_scatter | solution.py:234
  763.4 228.3 %reduce-scatter.21.cloned.1.call-start = ((), (), s32[]{:S(2)}) async-start(), calls=%async_computation.21 | async-start | bytes 5242880 | tf_op jit(solution)/shard_map/reduce_scatter | solution.py:228
  777.6 217.6 %reduce-scatter.19.cloned.1.call-start = ((), (), s32[]{:S(2)}) async-start(), calls=%async_computation.20 | async-start | bytes 1310720 | tf_op jit(solution)/shard_map/reduce_scatter | solution.py:231
  958.5 98.4 %reduce-scatter.17.cloned.1.call-start = ((), (), s32[]{:S(2)}) async-start(), calls=%async_computation.19 | async-start | bytes 3932160 | tf_op jit(solution)/shard_map/reduce_scatter | solution.py:225
  991.7 136.7 %all-reduce.8.cloned.1.call-start = ((), (), s32[]{:S(2)}) async-start(), calls=%async_computation.23 | async-start | bytes 6291456 | tf_op jit(solution)/shard_map/psum | solution.py:219
  1056.9 128.0 %reduce-scatter.15.cloned.1.call-start = ((), (), s32[]{:S(2)}) async-start(), calls=%async_computation.18 | async-start | bytes 6291456 | tf_op jit(solution)/shard_map/reduce_scatter | solution.py:56
  (48 other events, 436.7 us)
Sparse Core Ops, SparseCore 0:
  31.5 56.9 all-gather.7
  90.1 63.4 all-gather.9
  155.2 28.8 all-gather.11
  265.5 97.8 reduce-scatter.8
  364.9 101.6 all-gather.15
  468.0 59.2 all-gather.13
  529.0 56.7 all-gather.17
  626.8 53.5 reduce-scatter.12
  682.7 54.3 reduce-scatter.10
  749.0 56.8 all-gather.19
  808.3 76.7 reduce-scatter.22
  887.2 77.2 reduce-scatter.20
  967.5 27.6 reduce-scatter.18
  997.9 58.8 reduce-scatter.16
  1059.3 68.9 all-reduce.7
  1130.5 54.3 reduce-scatter.14
